TPU v7x, 256 devices: a whole 4x4x8 slice. The times are simulated.
256 devices in a mesh: img: 64 (over x, z, core), grp: 4 (over y).
Axes of the slice: x: 4, y: 4, z: 8, core: 2. Of those that a mesh axis runs over, the one named last changes fastest.
Arguments:
- desc: bfloat16 [256, 1024, 256], P(('img', 'grp')), may hold values from -20 to 20
- w_proj: bfloat16 [256, 512], replicated, may hold values from -0.375 to 0.375
- w_out: bfloat16 [256, 256], replicated, may hold values from -0.375 to 0.375
- pair_list: int32 [1280, 2], P(('img', 'grp')), may hold values from 0 to 255, as said below
- pair_count: int32 [256], P(('img', 'grp')), may hold values from 1 to 5, as said below
Outputs:
- updated: bfloat16 [256, 1024, 256], P(('img', 'grp'))
Inputs may be any that keep to these rules, and one draw needn't show every extreme that they name: `pair_list`: for a slot of the device at img index i, the first image lies in column i (ids i * 4 to i * 4 + 3) and the second in column i or column (i + 1) % 64, and the two ids differ; every slot holds such a pair, live or not. `pair_count`: some device has all 5 slots live.
All inputs are finite; a program needn't handle non-finite values.
Results may differ from a plain program's by a relative error of at most 0.0072.
Values may be sent and summed in bfloat16 or wider, within the bound.
No kernel may reach another device: no remote copies, remote signals or barrier semaphores. Data moves between devices by JAX's collectives and lax.ppermute only.
A program may use at most 64 MiB of HBM per device.

v0:
```python
import jax
import jax.numpy as jnp
from jax import lax
from jax.sharding import PartitionSpec as P

D = 256
HEADS = 4
HEAD_DIM = 64


def from_behind(block, axis, distance):
    devices = range(lax.axis_size(axis))
    route = [((i - distance) % len(devices), i) for i in devices]
    return lax.ppermute(block, axis, route)


def pair_messages(first_rows, second_rows):
    to_first = []
    to_second = []
    for head_index in range(HEADS):
        lower = head_index * HEAD_DIM
        query_first = first_rows[:, lower : lower + HEAD_DIM]
        query_second = second_rows[:, lower : lower + HEAD_DIM]
        value_first = first_rows[:, D + lower : D + lower + HEAD_DIM]
        value_second = second_rows[:, D + lower : D + lower + HEAD_DIM]
        scores = jnp.dot(
            query_first, query_second.T, preferred_element_type=jnp.float32
        ) * HEAD_DIM ** (-0.5)
        across = jnp.exp(scores - jnp.max(scores, axis=1, keepdims=True))
        across = (across / jnp.sum(across, axis=1, keepdims=True)).astype(jnp.bfloat16)
        downward = jnp.exp(scores - jnp.max(scores, axis=0, keepdims=True))
        downward = (downward / jnp.sum(downward, axis=0, keepdims=True)).astype(jnp.bfloat16)
        to_first.append(jnp.dot(across, value_second, preferred_element_type=jnp.float32))
        to_second.append(
            lax.dot_general(
                downward, value_first, (((0,), (0,)), ((), ())), preferred_element_type=jnp.float32
            )
        )
    return (
        jnp.concatenate(to_first, 1).astype(jnp.bfloat16),
        jnp.concatenate(to_second, 1).astype(jnp.bfloat16),
    )


def window_slot(image_ids, column_index, columns, members):
    return (image_ids // members - column_index) % columns * members + image_ids % members


def on_device(desc, w_proj, w_out, pair_list, pair_count):
    columns = lax.axis_size("img")
    members = lax.axis_size("grp")
    column_index = lax.axis_index("img")
    keypoints = desc.shape[1]
    own_rows = jnp.dot(desc[0], w_proj, preferred_element_type=jnp.float32).astype(jnp.bfloat16)[
        None
    ]
    group_rows = lax.all_gather(own_rows, "grp", axis=0, tiled=True)
    next_rows = from_behind(group_rows, "img", -1)
    window = jnp.concatenate([group_rows, next_rows], 0)
    live_count = pair_count[0]
    slots = window_slot(pair_list, column_index, columns, members)

    def visit(position, totals):
        first_slot = slots[position, 0]
        second_slot = slots[position, 1]
        first_rows = lax.dynamic_index_in_dim(window, first_slot, 0, keepdims=False)
        second_rows = lax.dynamic_index_in_dim(window, second_slot, 0, keepdims=False)
        to_first, to_second = pair_messages(first_rows, second_rows)
        totals = totals.at[first_slot].add(to_first.astype(jnp.float32))
        return totals.at[second_slot].add(to_second.astype(jnp.float32))

    totals = jnp.zeros((2 * members, keypoints, D), jnp.float32)
    totals = lax.fori_loop(0, live_count, visit, totals)
    returned = from_behind(totals[members:], "img", 1)
    summed = lax.psum_scatter(totals[:members] + returned, "grp", scatter_dimension=0, tiled=True)
    message = summed[0].astype(jnp.bfloat16)
    update = jnp.dot(message, w_out, preferred_element_type=jnp.float32)
    return (desc[0].astype(jnp.float32) + update).astype(jnp.bfloat16)[None]


def solution(mesh):
    return jax.shard_map(
        on_device,
        mesh=mesh,
        in_specs=(
            P(("img", "grp"), None, None),
            P(),
            P(),
            P(("img", "grp"), None),
            P(("img", "grp")),
        ),
        out_specs=P(("img", "grp"), None, None),
        check_vma=False,
    )
```

profile of v0, /device:TPU:1, one launch (start us, length us, event | category | flops | bytes accessed | tf_op | source)
XLA Modules:
  0.0 399.2 jit_solution(12478828602547499768)
XLA Ops:
  7.5 2.5 convolution_convert_fusion
  10.0 54.8 %all-gather.3.cloned.1.call-done = bf16[4096,512]{1,0:T(8,128)(2,1)} async-done(((bf16[1024,512]{1,0:T(8,128)(2,1)}), bf16[4096,512]{1,0:T(8,128)(2,1)}) %all-gather.3.cloned.1.call-update) | async-done | bytes 4194320 | tf_op jit(solution)/shard_map/all_gather | solution.py:57
  66.2 47.0 %collective-permute-done = bf16[4,1024,512]{2,1,0:T(8,128)(2,1)} collective-permute-done((bf16[4,1024,512]{2,1,0:T(8,128)(2,1)}, bf16[4,1024,512]{2,1,0:T(8,128)(2,1)}, u32[]{:S(2)}, u32[]{:S(2)}) %collective-permute-start) | collective-permute-done | bytes 4194336 | tf_op jit(solution)/shard_map/ppermute | solution.py:14
  113.1 7.4 %pad_maximum_fusion = bf16[8,1024,512]{2,1,0:T(8,128)(2,1)} fusion(bf16[4,1024,512]{2,1,0:T(8,128)(2,1)} %collective-permute-done, bf16[4,1024,512]{2,1,0:T(8,128)(2,1)} %bitcast.64), kind=kLoop, calls=%fused_computation.98 | loop fusion | flops 4194304 | bytes 16777216 | tf_op jit(solution)/shard_map/concatenate | solution.py:59
  120.5 4.3 %broadcast_in_dim.6 = f32[8,1024,256]{1,2,0:T(8,128)} broadcast(f32[]{:T(128)} %constant.102.clone.1), dimensions={} | broadcast | bytes 8388612 | tf_op jit(solution)/shard_map/broadcast_in_dim | solution.py:72
  124.8 65.9 %while.12 = (s32[]{:T(128)}, f32[8,1024,256]{1,2,0:T(8,128)}, s32[]{:T(128)}, s32[5,2]{0,1:T(2,128)S(1)}, bf16[8,1024,512]{2,1,0:T(8,128)(2,1)}, /*index=5*/s32[...) while((s32[]{:T(128)}, f32[8,1024,256]{1,2,0:T(8,128)}, s32[]{:T(128)}, ...), condition=%wide.region_19.20_spmd, body=%wide.region_0.19_spmd.sunk | while | flops 1683472384 | bytes 81955088 | solution.py:73
  131.0 1.7 dynamic-slice_bitcast_fusion.3
  133.5 1.6 fusion.108
  135.0 1.3 fusion.109
  138.2 1.6 fusion.106
  139.7 1.2 fusion.107
  142.8 1.6 fusion.104
  144.3 1.2 fusion.105
  147.4 1.6 fusion.102
  150.0 1.2 fusion.103
  151.3 3.0 fusion.110
  154.3 3.1 fusion.115
  163.5 1.7 dynamic-slice_bitcast_fusion.3
  165.9 1.6 fusion.108
  167.5 1.3 fusion.109
  170.6 1.6 fusion.106
  172.2 1.2 fusion.107
  175.2 1.6 fusion.104
  179.9 1.6 fusion.102
  182.5 1.2 fusion.103
  183.7 3.0 fusion.110
  186.8 3.1 fusion.115
  190.8 2.7 slice.93
  193.5 45.4 %collective-permute-done.1 = f32[4,1024,256]{1,2,0:T(8,128)S(1)} collective-permute-done((f32[4,1024,256]{1,2,0:T(8,128)S(1)}, f32[4,1024,256]{1,2,0:T(8,128)S(1)}, u32[]{:S(2)}, u32[]{:S(2)}) %collective-permute-start.1) | collective-permute-done | bytes 4194336 | tf_op jit(solution)/shard_map/ppermute | solution.py:14
  239.0 2.9 slice_add_fusion
  241.8 148.2 %reduce-scatter.2.cloned.1.call-done = f32[1,1024,256]{1,2,0:T(8,128)} async-done(((f32[4,1024,256]{1,2,0:T(8,128)}), f32[1,1024,256]{1,2,0:T(8,128)}) %reduce-scatter.2.cloned.1.call-update) | async-done | bytes 1048592 | tf_op jit(solution)/shard_map/reduce_scatter | solution.py:75
  390.0 2.4 fusion.63
  (38 shorter events, 21.4 us)
Async XLA Ops:
  6.5 1.0 copy-start
  6.5 58.2 %all-gather.3.cloned.1.call-start = ((), (), s32[]{:S(2)}) async-start(), calls=%async_computation.2 | async-start | bytes 5242880 | tf_op jit(solution)/shard_map/all_gather | solution.py:57
  10.0 380.1 %reduce-scatter.2.cloned.1.call-start = ((), (), s32[]{:S(2)}) async-start(), calls=%async_computation.1 | async-start | bytes 5242880 | tf_op jit(solution)/shard_map/reduce_scatter | solution.py:75
  64.8 48.3 %collective-permute-start = (bf16[4,1024,512]{2,1,0:T(8,128)(2,1)}, bf16[4,1024,512]{2,1,0:T(8,128)(2,1)}, u32[]{:S(2)}, u32[]{:S(2)}) collective-permute-start(bf16[4,1024,512]{2,1,0:T(8,128)(2,1)} %bitcast.63), channel_id=1, source_target_pairs={{4,0},{8,4},{12,8},{16,12},{20,16},{24,20},{28,24},{32,28},{36,32}... | collective-permute-start | bytes 12582920 | tf_op jit(solution)/shard_map/ppermute | solution.py:14
  120.5 4.3 %copy-start.4 = (s32[3]{0:T(128)S(1)}, s32[3]{0:T(128)}, u32[]{:S(2)}) copy-start(s32[3]{0:T(128)} %constant.96.clone.1) | copy-start | bytes 40
  190.8 48.2 %copy-start.1 = (f32[8,1024,256]{1,2,0:T(8,128)S(1)}, f32[8,1024,256]{1,2,0:T(8,128)}, u32[]{:S(2)}) copy-start(f32[8,1024,256]{1,2,0:T(8,128)} %get-tuple-element.57) | copy-start | bytes 25165828
  193.4 45.5 %collective-permute-start.1 = (f32[4,1024,256]{1,2,0:T(8,128)S(1)}, f32[4,1024,256]{1,2,0:T(8,128)S(1)}, u32[]{:S(2)}, u32[]{:S(2)}) collective-permute-start(f32[4,1024,256]{1,2,0:T(8,128)S(1)} %slice.93), channel_id=1, source_target_pairs={{252,0},{0,4},{4,8},{8,12},{12,16},{16,20},{20,24},{24,28},{28,32}... | collective-permute-start | bytes 12582920 | tf_op jit(solution)/shard_map/ppermute | solution.py:14
  241.8 148.2 %copy-start.2 = (bf16[1,1024,256]{2,1,0:T(8,128)(2,1)S(1)}, bf16[1,1024,256]{2,1,0:T(8,128)(2,1)}, u32[]{:S(2)}) copy-start(bf16[1,1024,256]{2,1,0:T(8,128)(2,1)} %param.11) | copy-start | bytes 1572868
  241.8 148.2 %copy-start.3 = (bf16[256,256]{1,0:T(8,128)(2,1)S(1)}, bf16[256,256]{1,0:T(8,128)(2,1)}, u32[]{:S(2)}) copy-start(bf16[256,256]{1,0:T(8,128)(2,1)} %param.13) | copy-start | bytes 393220
Sparse Core Ops, SparseCore 0:
  10.1 54.6 all-gather.2
  242.0 148.0 reduce-scatter.1
where the time goes:
time: 400 us; the launch traced here: 399 us
  waiting for transfers between devices  295 us (74%)
  other arithmetic  37.2 us (9%)
  matrix products  29.6 us (7%)
  between operations  13.4 us (3%)
  local copies, waits for them, and re-layouts  12.6 us (3%)
  loops' own time  10.2 us (3%)
    reduce_scatter x1, waiting for transfers between devices, on_device(): lax.psum_scatter(totals[:members] + returned, 'grp', scatter_dimension=0,...  148 us
    ppermute x2, waiting for transfers between devices, from_behind(): return lax.ppermute(block, axis, route)  92.4 us
    all_gather x1, waiting for transfers between devices, on_device(): group_rows = lax.all_gather(own_rows, 'grp', axis=0, tiled=True)  54.8 us
    reduce_sum x8, other arithmetic, pair_messages(): jnp.sum(downward, axis=0, keepdims=True)  12.4 us
    another operation x1, loops' own time, on_device(): totals = lax.fori_loop(0, live_count, visit, totals)  10.2 us
    dot_general x8, matrix products, pair_messages(): jnp.dot(across, value_second, preferred_element_type=jnp.float32)  9.98 us
    dot_general x8, matrix products, pair_messages(): lax.dot_general(downward, value_first, (((0,), (0,)), ((), ())), preferre...  8.13 us
  transfers between devices with their start and end apart: 4, of which 4 were waited for; matrix products, arithmetic and copies ran while one was open for 0% of the time, Pallas kernels for 0%

commit v1 on v0

--- a/solution.py
+++ b/solution.py
@@ -54,7 +54,9 @@
     own_rows = jnp.dot(desc[0], w_proj, preferred_element_type=jnp.float32).astype(jnp.bfloat16)[
         None
     ]
-    group_rows = lax.all_gather(own_rows, "grp", axis=0, tiled=True)
+    group_rows = jnp.concatenate(
+        lax.all_to_all(jnp.stack([own_rows] * lax.axis_size("grp")), "grp", 0, 0), axis=0
+    )
     next_rows = from_behind(group_rows, "img", -1)
     window = jnp.concatenate([group_rows, next_rows], 0)
     live_count = pair_count[0]

time: 400 us -> 401 us (level)
  waiting for transfers between devices: 295 us -> 243 us
  blocking collectives: 0 us -> 51.9 us
    all_gather x1 -> x0, waiting for transfers between devices: 54.8 us -> none  [on_device(): group_rows = lax.all_gather(own_rows, 'grp', axis=0, tiled=True)]
    all_to_all x0 -> x1, blocking collectives: none -> 51.9 us  [on_device(): lax.all_to_all(jnp.stack([own_rows] * lax.axis_size('grp')), 'grp', 0, 0)]
  transfers between devices with their start and end apart: 4 -> 3, of which waited for: 4 -> 3; matrix products, arithmetic and copies ran while one was open for 0% -> 0% of each run, Pallas kernels for 0% -> 0%
where the time goes in v1:
time: 401 us; the launch traced here: 399 us
  waiting for transfers between devices  243 us (61%)
  blocking collectives  51.9 us (13%)
  other arithmetic  36.6 us (9%)
  matrix products  28.6 us (7%)
  between operations  13.5 us (3%)
  local copies, waits for them, and re-layouts  12.9 us (3%)
  loops' own time  10.2 us (3%)
    reduce_scatter x1, waiting for transfers between devices, on_device(): lax.psum_scatter(totals[:members] + returned, 'grp', scatter_dimension=0,...  149 us
    ppermute x2, waiting for transfers between devices, from_behind(): return lax.ppermute(block, axis, route)  93.4 us
    all_to_all x1, blocking collectives, on_device(): lax.all_to_all(jnp.stack([own_rows] * lax.axis_size('grp')), 'grp', 0, 0)  51.9 us
    reduce_sum x8, other arithmetic, pair_messages(): jnp.sum(downward, axis=0, keepdims=True)  12.4 us
    another operation x1, loops' own time, on_device(): totals = lax.fori_loop(0, live_count, visit, totals)  10.2 us
    dot_general x8, matrix products, pair_messages(): jnp.dot(across, value_second, preferred_element_type=jnp.float32)  9.99 us
    dot_general x8, matrix products, pair_messages(): lax.dot_general(downward, value_first, (((0,), (0,)), ((), ())), preferre...  8.13 us
  transfers between devices with their start and end apart: 3, of which 3 were waited for; matrix products, arithmetic and copies ran while one was open for 0% of the time, Pallas kernels for 0%

profile of v1, /device:TPU:1, one launch (start us, length us, event | category | flops | bytes accessed | tf_op | source)
XLA Modules:
  0.0 399.3 jit_solution(6498036633131855511)
XLA Ops:
  7.5 1.5 convolution_convert_fusion
  9.3 51.9 %all_to_all.5 = bf16[4,1,1024,512]{3,2,1,0:T(8,128)(2,1)} all-to-all(bf16[4,1,1024,512]{3,2,1,0:T(8,128)(2,1)S(1)} %stack.3), channel_id=1, replica_groups=mesh['img'=64,'grp'=4] {'grp'}, dimensions={0} | all-to-all | bytes 8388608 | tf_op jit(solution)/shard_map/all_to_all | solution.py:58
  61.2 2.7 collective-permute-start
  64.0 48.0 %collective-permute-done = bf16[4,1024,512]{2,1,0:T(8,128)(2,1)} collective-permute-done((bf16[4,1024,512]{2,1,0:T(8,128)(2,1)}, bf16[4,1024,512]{2,1,0:T(8,128)(2,1)}, u32[]{:S(2)}, u32[]{:S(2)}) %collective-permute-start) | collective-permute-done | bytes 4194336 | tf_op jit(solution)/shard_map/ppermute | solution.py:14
  112.0 7.4 %pad_maximum_fusion = bf16[8,1024,512]{2,1,0:T(8,128)(2,1)} fusion(bf16[4,1024,512]{2,1,0:T(8,128)(2,1)} %collective-permute-done, bf16[4,1024,512]{2,1,0:T(8,128)(2,1)} %bitcast.16), kind=kLoop, calls=%fused_computation.98 | loop fusion | flops 4194304 | bytes 16777216 | tf_op jit(solution)/shard_map/concatenate | solution.py:61
  119.4 4.3 %broadcast_in_dim.4 = f32[8,1024,256]{1,2,0:T(8,128)} broadcast(f32[]{:T(128)} %constant.102.clone.1), dimensions={} | broadcast | bytes 8388612 | tf_op jit(solution)/shard_map/broadcast_in_dim | solution.py:74
  123.7 65.9 %while.12 = (s32[]{:T(128)}, f32[8,1024,256]{1,2,0:T(8,128)}, s32[]{:T(128)}, s32[5,2]{0,1:T(2,128)S(1)}, bf16[8,1024,512]{2,1,0:T(8,128)(2,1)}, /*index=5*/s32[...) while((s32[]{:T(128)}, f32[8,1024,256]{1,2,0:T(8,128)}, s32[]{:T(128)}, ...), condition=%wide.region_19.20_spmd, body=%wide.region_0.19_spmd.sunk | while | flops 1683472384 | bytes 81955088 | solution.py:75
  129.9 1.7 dynamic-slice_bitcast_fusion.3
  132.4 1.6 fusion.108
  133.9 1.3 fusion.109
  137.0 1.6 fusion.106
  138.6 1.2 fusion.107
  141.7 1.6 fusion.104
  143.2 1.2 fusion.105
  146.3 1.6 fusion.102
  148.9 1.2 fusion.103
  150.2 3.0 fusion.110
  153.2 3.1 fusion.115
  162.3 1.7 dynamic-slice_bitcast_fusion.3
  164.8 1.6 fusion.108
  166.4 1.3 fusion.109
  169.5 1.6 fusion.106
  174.1 1.6 fusion.104
  178.8 1.6 fusion.102
  181.4 1.2 fusion.103
  182.6 3.0 fusion.110
  185.7 3.1 fusion.115
  189.6 2.7 slice.93
  192.4 45.4 %collective-permute-done.1 = f32[4,1024,256]{1,2,0:T(8,128)S(1)} collective-permute-done((f32[4,1024,256]{1,2,0:T(8,128)S(1)}, f32[4,1024,256]{1,2,0:T(8,128)S(1)}, u32[]{:S(2)}, u32[]{:S(2)}) %collective-permute-start.1) | collective-permute-done | bytes 4194336 | tf_op jit(solution)/shard_map/ppermute | solution.py:14
  237.8 2.9 slice_add_fusion
  240.7 149.4 %reduce-scatter.2.cloned.1.call-done = f32[1,1024,256]{1,2,0:T(8,128)} async-done(((f32[4,1024,256]{1,2,0:T(8,128)}), f32[1,1024,256]{1,2,0:T(8,128)}) %reduce-scatter.2.cloned.1.call-update) | async-done | bytes 1048592 | tf_op jit(solution)/shard_map/reduce_scatter | solution.py:77
  390.1 2.4 fusion.63
  (39 shorter events, 21.6 us)
Async XLA Ops:
  6.5 1.0 copy-start
  6.5 383.6 %reduce-scatter.2.cloned.1.call-start = ((), (), s32[]{:S(2)}) async-start(), calls=%async_computation.2 | async-start | bytes 5242880 | tf_op jit(solution)/shard_map/reduce_scatter | solution.py:77
  9.3 54.7 %copy-start.5 = (s32[5,2]{0,1:T(2,128)S(1)}, s32[5,2]{0,1:T(2,128)}, u32[]{:S(2)}) copy-start(s32[5,2]{0,1:T(2,128)} %param.14) | copy-start | bytes 124
  61.2 50.8 %collective-permute-start = (bf16[4,1024,512]{2,1,0:T(8,128)(2,1)}, bf16[4,1024,512]{2,1,0:T(8,128)(2,1)}, u32[]{:S(2)}, u32[]{:S(2)}) collective-permute-start(bf16[4,1024,512]{2,1,0:T(8,128)(2,1)} %bitcast.16), channel_id=1, source_target_pairs={{4,0},{8,4},{12,8},{16,12},{20,16},{24,20},{28,24},{32,28},{36,32}... | collective-permute-start | bytes 12582920 | tf_op jit(solution)/shard_map/ppermute | solution.py:14
  119.4 4.3 %copy-start.4 = (s32[3]{0:T(128)S(1)}, s32[3]{0:T(128)}, u32[]{:S(2)}) copy-start(s32[3]{0:T(128)} %constant.96.clone.1) | copy-start | bytes 40
  189.6 48.2 %copy-start.1 = (f32[8,1024,256]{1,2,0:T(8,128)S(1)}, f32[8,1024,256]{1,2,0:T(8,128)}, u32[]{:S(2)}) copy-start(f32[8,1024,256]{1,2,0:T(8,128)} %get-tuple-element.57) | copy-start | bytes 25165828
  192.3 45.5 %collective-permute-start.1 = (f32[4,1024,256]{1,2,0:T(8,128)S(1)}, f32[4,1024,256]{1,2,0:T(8,128)S(1)}, u32[]{:S(2)}, u32[]{:S(2)}) collective-permute-start(f32[4,1024,256]{1,2,0:T(8,128)S(1)} %slice.93), channel_id=1, source_target_pairs={{252,0},{0,4},{4,8},{8,12},{12,16},{16,20},{20,24},{24,28},{28,32}... | collective-permute-start | bytes 12582920 | tf_op jit(solution)/shard_map/ppermute | solution.py:14
  240.7 149.4 %copy-start.2 = (bf16[1,1024,256]{2,1,0:T(8,128)(2,1)S(1)}, bf16[1,1024,256]{2,1,0:T(8,128)(2,1)}, u32[]{:S(2)}) copy-start(bf16[1,1024,256]{2,1,0:T(8,128)(2,1)} %param.11) | copy-start | bytes 1572868
  240.7 149.4 %copy-start.3 = (bf16[256,256]{1,0:T(8,128)(2,1)S(1)}, bf16[256,256]{1,0:T(8,128)(2,1)}, u32[]{:S(2)}) copy-start(bf16[256,256]{1,0:T(8,128)(2,1)} %param.13) | copy-start | bytes 393220
Sparse Core Ops, SparseCore 0:
  240.9 149.2 reduce-scatter.1
